TPU v7x, 32 devices: a whole 2x2x4 slice. The times are simulated.
32 devices in a mesh: space: 8 (over z, x), vel: 4 (over y, core).
Axes of the slice: x: 2, y: 2, z: 4, core: 2. Of those that a mesh axis runs over, the one named last changes fastest.
Arguments:
- probe_field: float32 [2, 1024, 1024], P(None, 'space'), may hold values from -6 to 6
- control_field: float32 [2, 1024, 1024], P(None, 'space'), may hold values from -4 to 4
- optical_state: float32 [2, 64, 1024, 1024], P(None, 'vel', 'space'), may hold values from -3 to 3
- spin_state: float32 [2, 64, 1024, 1024], P(None, 'vel', 'space'), may hold values from -3 to 3
- doppler_shift: float32 [64], P('vel'), may hold values from -3 to 3
- class_weight: float32 [64], P('vel'), may hold values from 0.2 to 2
- gradient_shift: float32 [1024, 1024], P('space'), may hold values from -3 to 3
Outputs:
- probe_out: float32 [2, 1024, 1024], P(None, 'space')
- control_out: float32 [2, 1024, 1024], P(None, 'space')
- optical_out: float32 [2, 64, 1024, 1024], P(None, 'vel', 'space')
- spin_out: float32 [2, 64, 1024, 1024], P(None, 'vel', 'space')
All inputs are finite; a program needn't handle non-finite values.
Results may differ from a plain program's by a relative error of at most 0.000098.
Values sent between devices are 32-bit elements; how exact they have to be, the bound alone decides.
A program may use at most 192 MiB of HBM per device.

v0:
```python
import jax
import jax.numpy as jnp
import numpy as np
from jax import lax
from jax.sharding import PartitionSpec as P

GRID = 1024
VEL = 64


GAMMA = 1.0
DEPHASE = 0.1
DT = 0.25
COUPLE = 2.0
HIGHEST = lax.Precision.HIGHEST


def circulant_tables(grid_width):
    counter = np.arange(grid_width, dtype=np.int32)
    frequency = np.where(counter < grid_width // 2, counter, counter - grid_width)
    angles = (
        np.float32(np.pi)
        * (frequency * frequency % (2 * grid_width)).astype(np.float32)
        / np.float32(grid_width)
    )
    turns = counter[:, None] * counter[None, :] % grid_width
    argument = (
        np.float32(2.0 * np.pi) * turns.astype(np.float32) / np.float32(grid_width)
        - angles[None, :]
    )
    kernel_real = np.mean(np.cos(argument), axis=1)
    kernel_imag = np.mean(np.sin(argument), axis=1)
    offsets = (counter[:, None] - counter[None, :]) % grid_width
    return (kernel_real[offsets].astype(np.float32), kernel_imag[offsets].astype(np.float32))


def mix_left(table_real, table_imag, section):
    real_in, imag_in = (section[:, 0], section[:, 1])

    def product_of(table, values):
        return jnp.einsum("mn,fnk->fmk", table, values, precision=HIGHEST)

    return jnp.stack(
        [
            product_of(table_real, real_in) - product_of(table_imag, imag_in),
            product_of(table_real, imag_in) + product_of(table_imag, real_in),
        ],
        axis=1,
    )


def mix_right(section, table_real, table_imag):
    real_in, imag_in = (section[:, 0], section[:, 1])

    def product_of(values, table):
        return jnp.einsum("fmn,nk->fmk", values, table, precision=HIGHEST)

    return jnp.stack(
        [
            product_of(real_in, table_real) - product_of(imag_in, table_imag),
            product_of(imag_in, table_real) + product_of(real_in, table_imag),
        ],
        axis=1,
    )


def derivative(optical, spin_part, probe_part, control, doppler, gradient):
    optical_real, optical_imag = (optical[0], optical[1])
    spin_real, spin_imag = (spin_part[0], spin_part[1])
    probe_real, probe_imag = (probe_part[0], probe_part[1])
    control_real, control_imag = (control[0], control[1])
    rate_optical_real = (
        -GAMMA * optical_real
        + doppler * optical_imag
        - probe_imag
        - (control_real * spin_imag + control_imag * spin_real)
    )
    rate_optical_imag = (
        -GAMMA * optical_imag
        - doppler * optical_real
        + probe_real
        + (control_real * spin_real - control_imag * spin_imag)
    )
    rate_spin_real = (
        -DEPHASE * spin_real
        + gradient * spin_imag
        - (control_real * optical_imag - control_imag * optical_real)
    )
    rate_spin_imag = (
        -DEPHASE * spin_imag
        - gradient * spin_real
        + (control_real * optical_real + control_imag * optical_imag)
    )
    return (
        jnp.stack([rate_optical_real, rate_optical_imag]),
        jnp.stack([rate_spin_real, rate_spin_imag]),
    )


def midpoint(optical, spin_part, probe_part, control, doppler, gradient):
    rate_optical, rate_spin = derivative(optical, spin_part, probe_part, control, doppler, gradient)
    half_optical = optical + 0.5 * DT * rate_optical
    half_spin = spin_part + 0.5 * DT * rate_spin
    rate_optical, rate_spin = derivative(
        half_optical, half_spin, probe_part, control, doppler, gradient
    )
    return (optical + DT * rate_optical, spin_part + DT * rate_spin)


def add_source(complex_field, polarization):
    return jnp.stack(
        [complex_field[0] - COUPLE * polarization[1], complex_field[1] + COUPLE * polarization[0]]
    )


def shards(
    probe_field,
    control_field,
    optical_state,
    spin_state,
    doppler_shift,
    class_weight,
    gradient_shift,
):
    grid_width = GRID
    quarter_width = grid_width // lax.axis_size("vel")
    table_real, table_imag = circulant_tables(grid_width)
    full_real = jnp.asarray(table_real)
    full_imag = jnp.asarray(table_imag)

    def row_mix(section):
        blended = mix_left(
            full_real,
            full_imag,
            lax.all_to_all(section, "space", split_axis=3, concat_axis=2, tiled=True),
        )
        return lax.all_to_all(blended, "space", split_axis=2, concat_axis=3, tiled=True)

    def spread(section):
        return lax.all_gather(section, "vel", axis=3, tiled=True)

    stacked = jnp.stack([probe_field, control_field])
    col_start = lax.axis_index("vel") * quarter_width
    quart_real = lax.dynamic_slice_in_dim(full_real, col_start, quarter_width, 1)
    quart_imag = lax.dynamic_slice_in_dim(full_imag, col_start, quarter_width, 1)
    stacked = spread(row_mix(mix_right(stacked, quart_real, quart_imag)))
    optical_new, spin_new = midpoint(
        optical_state,
        spin_state,
        stacked[0],
        stacked[1],
        doppler_shift[:, None, None],
        gradient_shift,
    )
    weighted = jnp.einsum("cvrn,v->crn", optical_new, class_weight, precision=HIGHEST) / VEL
    polarization = lax.psum_scatter(weighted, "vel", scatter_dimension=2, tiled=True)
    probe_part = lax.dynamic_slice_in_dim(stacked[0], col_start, quarter_width, 2)
    control_part = lax.dynamic_slice_in_dim(stacked[1], col_start, quarter_width, 2)
    section = jnp.stack([add_source(probe_part, polarization), control_part])
    stacked = mix_right(spread(row_mix(section)), full_real, full_imag)
    return (stacked[0], stacked[1], optical_new, spin_new)


def solution(mesh):
    return jax.shard_map(
        shards,
        mesh=mesh,
        in_specs=(
            P(None, "space", None),
            P(None, "space", None),
            P(None, "vel", "space", None),
            P(None, "vel", "space", None),
            P("vel"),
            P("vel"),
            P("space", None),
        ),
        out_specs=(
            P(None, "space", None),
            P(None, "space", None),
            P(None, "vel", "space", None),
            P(None, "vel", "space", None),
        ),
        check_vma=False,
    )
```

profile of v0, /device:TPU:0, one launch (start us, length us, event | category | flops | bytes accessed | tf_op | source)
XLA Modules:
  0.0 411.2 jit_solution(229504936186904210)
XLA Ops:
  17.8 21.6 %all_to_all.72 = f32[2,2,128,256]{2,0,1,3:T(2,128)S(1)} all-to-all(f32[2,2,128,256]{2,0,1,3:T(2,128)S(1)} %copy.38), channel_id=1, replica_groups=mesh['space'=8,'vel'=4] {'space'}, dimensions={3} | all-to-all | bytes 1048576 | tf_op jit(solution)/shard_map/all_to_all | solution.py:135
  39.9 6.4 %fusion.35 = f32[2,32,1024]{2,1,0:T(8,128)S(1)} fusion(f32[1024,1024,1]{1,0,2:T(8,128)} %constant.31, f32[2,2,1024,32]{2,3,0,1:T(8,128)S(1)} %all_to_all.55), kind=kOutput, calls=%fused_computation.75 | convolution fusion | flops 805306368 | bytes 4718592 | tf_op jit(solution)/shard_map/mn,fnk->fmk/dot_general | solution.py:41
  46.3 6.3 %fusion.34 = f32[2,32,1024]{2,1,0:T(8,128)S(1)} fusion(f32[1024,1024,1]{1,0,2:T(8,128)} %constant.31, f32[2,2,1024,32]{2,3,0,1:T(8,128)S(1)} %all_to_all.55), kind=kOutput, calls=%fused_computation.74 | convolution fusion | flops 805306368 | bytes 4718592 | tf_op jit(solution)/shard_map/mn,fnk->fmk/dot_general | solution.py:41
  52.5 4.1 %fusion.10 = f32[2,1,1024,32]{2,3,0,1:T(8,128)S(1)} fusion(f32[2,32,1024]{2,1,0:T(8,128)S(1)} %fusion.35, f32[1024,1024,1]{1,0,2:T(8,128)S(1)} %copy-done.1, f32[2,2,1024,32]{2,3,0,1:T(8,128)S(1)} %all_to_all.55), kind=kOutput, calls=%fused_computation.31 | convolution fusion | flops 805371904 | bytes 4980736 | tf_op jit(solution)/shard_map/mn,fnk->fmk/dot_general | solution.py:41
  56.6 4.6 %fusion.11 = f32[2,1,1024,32]{2,3,0,1:T(8,128)S(1)} fusion(f32[2,32,1024]{2,1,0:T(8,128)S(1)} %fusion.34, f32[1024,1024,1]{1,0,2:T(8,128)S(1)} %copy-done.1, f32[2,2,1024,32]{2,3,0,1:T(8,128)S(1)} %all_to_all.55), kind=kOutput, calls=%fused_computation.33 | convolution fusion | flops 805371904 | bytes 4980736 | tf_op jit(solution)/shard_map/mn,fnk->fmk/dot_general | solution.py:41
  64.8 17.7 %all_to_all.73 = f32[8,1,16384]{2,1,0:T(1,128)S(1)} all-to-all(f32[8,1,16384]{2,1,0:T(1,128)S(1)} %reshape.33), channel_id=1, replica_groups=mesh['space'=8,'vel'=4] {'space'}, dimensions={0} | all-to-all | bytes 1048576 | tf_op jit(solution)/shard_map/all_to_all | solution.py:137
  89.3 21.7 %all-gather.3.cloned.1.call-done = f32[2,2,128,1024]{2,3,1,0:T(8,128)} async-done(((f32[2,2,128,256]{2,3,1,0:T(8,128)}), f32[2,2,128,1024]{2,3,1,0:T(8,128)}) %all-gather.3.cloned.1.call-update) | async-done | bytes 2097168 | tf_op jit(solution)/shard_map/all_gather | solution.py:140
  113.5 18.6 %subtract_subtract_fusion.1 = (f32[1,16,128,1024]{3,2,1,0:T(8,128)}, f32[1,16,128,1024]{3,2,1,0:T(8,128)}) fusion(f32[2,16,128,1024]{3,2,1,0:T(8,128)} %param.12, f32[2,16,128,1024]{3,2,1,0:T(8,128)} %param.11, f32[128,1024]{1,0:T(8,128)S(1)} %copy-done.9, f32[128,1024]{1,0:T(8,128)S(1)} %copy.46, f32[128,1024]{1,0:T(8,128)S(1)} %copy.45), kind=kLoop, calls=%fused_computation.15 | loop fusion | flops 29360128 | bytes 51904512 | tf_op jit(solution)/shard_map/sub | solution.py:85
  132.1 18.4 %add_subtract_fusion.1 = (f32[1,16,128,1024]{3,2,1,0:T(8,128)}, f32[1,16,128,1024]{3,2,1,0:T(8,128)}) fusion(f32[2,16,128,1024]{3,2,1,0:T(8,128)} %param.12, f32[2,16,128,1024]{3,2,1,0:T(8,128)} %param.11, f32[128,1024]{1,0:T(8,128)S(1)} %copy.46, f32[128,1024]{1,0:T(8,128)S(1)} %copy.45, f32[128,1024]{1,0:T(8,128)S(1)} %copy.44, f32[16]{0:T(128)S(1)} %copy-done.10, ...), kind=kLoop, calls=%fused_computation.17 | loop fusion | flops 33554432 | bytes 52428864 | tf_op jit(solution)/shard_map/sub | solution.py:73
  150.5 33.9 %fusion = (f32[2,16,128,1024]{3,2,1,0:T(8,128)}, f32[2,16,128,1024]{3,2,1,0:T(8,128)}) fusion(f32[2,16,128,1024]{3,2,1,0:T(8,128)} %param.11, f32[1,16,128,1024]{3,2,1,0:T(8,128)} %get-tuple-element.11, f32[1,16,128,1024]{3,2,1,0:T(8,128)} %get-tuple-element.10, f32[2,16,128,1024]{3,2,1,0:T(8,128)} %param.12, f32[1,16,128,1024]{3,2,1,0:T(8,128)} %get-tuple-element.7, ...), kind=kLoop, calls=%fused_computation.1 | loop fusion | flops 25165824 | bytes 100663296 | tf_op jit(solution)/shard_map/add | solution.py:102
  184.4 18.4 %add_subtract_fusion = (f32[1,16,128,1024]{3,2,1,0:T(8,128)}, f32[1,16,128,1024]{3,2,1,0:T(8,128)}) fusion(f32[2,16,128,1024]{3,2,1,0:T(8,128)} %get-tuple-element.23, f32[2,16,128,1024]{3,2,1,0:T(8,128)} %get-tuple-element.22, f32[128,1024]{1,0:T(8,128)S(1)} %copy.46, f32[128,1024]{1,0:T(8,128)S(1)} %copy.45, f32[128,1024]{1,0:T(8,128)S(1)} %copy.44, ...), kind=kLoop, calls=%fused_computation.13 | loop fusion | flops 33554432 | bytes 52428864 | tf_op jit(solution)/shard_map/sub | solution.py:73
  202.7 11.9 %fusion.2 = f32[2,16,128,1024]{3,2,1,0:T(8,128)S(1)} fusion(f32[2,16,128,1024]{3,2,1,0:T(8,128)} %param.11, f32[1,16,128,1024]{3,2,1,0:T(8,128)} %get-tuple-element.9, f32[1,16,128,1024]{3,2,1,0:T(8,128)} %get-tuple-element.8), kind=kLoop, calls=%fused_computation.5 | loop fusion | flops 12582912 | bytes 50331648 | tf_op jit(solution)/shard_map/add | solution.py:107
  214.6 6.2 %copy-done.4 = f32[2,16,128,1024]{3,2,1,0:T(8,128)} copy-done((f32[2,16,128,1024]{3,2,1,0:T(8,128)}, f32[2,16,128,1024]{3,2,1,0:T(8,128)S(1)}, u32[]{:S(2)}) %copy-start.4) | copy-done | bytes 16777240
  220.8 16.7 %fusion.4 = f32[1,2,128,1024]{3,0,2,1:T(1,128)} fusion(f32[2,16,128,1024]{3,2,1,0:T(8,128)S(1)} %fusion.2, f32[16]{0:T(128)S(1)} %copy-done), kind=kOutput, calls=%fused_computation.8 | convolution fusion | flops 50331648 | bytes 17825856 | tf_op jit(solution)/shard_map/cvrn,v->crn/dot_general | solution.py:155
  244.6 23.8 %reduce-scatter.2.cloned.1.call-done = f32[2,128,256]{1,2,0:T(8,128)} async-done(((f32[2,128,1024]{1,2,0:T(8,128)}), f32[2,128,256]{1,2,0:T(8,128)}) %reduce-scatter.2.cloned.1.call-update) | async-done | bytes 262160 | tf_op jit(solution)/shard_map/reduce_scatter | solution.py:156
  270.0 19.7 %all_to_all.74 = f32[2,2,128,256]{2,1,0,3:T(2,128)S(1)} all-to-all(f32[2,2,128,256]{2,1,0,3:T(2,128)S(1)} %copy.48), channel_id=1, replica_groups=mesh['space'=8,'vel'=4] {'space'}, dimensions={3} | all-to-all | bytes 1048576 | tf_op jit(solution)/shard_map/all_to_all | solution.py:135
  290.1 6.4 %fusion.37 = f32[2,32,1024]{2,1,0:T(8,128)S(1)} fusion(f32[1024,1024,1]{1,0,2:T(8,128)} %constant.31, f32[2,2,1024,32]{2,3,0,1:T(8,128)S(1)} %all_to_all.63), kind=kOutput, calls=%fused_computation.77 | convolution fusion | flops 805306368 | bytes 4718592 | tf_op jit(solution)/shard_map/mn,fnk->fmk/dot_general | solution.py:41
  296.5 6.3 %fusion.36 = f32[2,32,1024]{2,1,0:T(8,128)S(1)} fusion(f32[1024,1024,1]{1,0,2:T(8,128)} %constant.31, f32[2,2,1024,32]{2,3,0,1:T(8,128)S(1)} %all_to_all.63), kind=kOutput, calls=%fused_computation.76 | convolution fusion | flops 805306368 | bytes 4718592 | tf_op jit(solution)/shard_map/mn,fnk->fmk/dot_general | solution.py:41
  306.9 4.3 %fusion.9 = f32[2,1,1024,32]{2,3,0,1:T(8,128)S(1)} fusion(f32[2,32,1024]{2,1,0:T(8,128)S(1)} %fusion.36, f32[1024,1024,1]{1,0,2:T(8,128)S(1)} %copy-done.2, f32[2,2,1024,32]{2,3,0,1:T(8,128)S(1)} %all_to_all.63), kind=kOutput, calls=%fused_computation.29 | convolution fusion | flops 805371904 | bytes 4980736 | tf_op jit(solution)/shard_map/mn,fnk->fmk/dot_general | solution.py:41
  317.7 17.7 %all_to_all.75 = f32[8,1,16384]{2,1,0:T(1,128)S(1)} all-to-all(f32[8,1,16384]{2,1,0:T(1,128)} %reshape.35), channel_id=1, replica_groups=mesh['space'=8,'vel'=4] {'space'}, dimensions={0} | all-to-all | bytes 1048576 | tf_op jit(solution)/shard_map/all_to_all | solution.py:137
  345.5 20.3 %subtract_subtract_fusion = (f32[1,16,128,1024]{3,2,1,0:T(8,128)}, f32[1,16,128,1024]{3,2,1,0:T(8,128)}) fusion(f32[2,16,128,1024]{3,2,1,0:T(8,128)} %get-tuple-element.23, f32[2,16,128,1024]{3,2,1,0:T(8,128)} %get-tuple-element.22, f32[128,1024]{1,0:T(8,128)} %param.15, f32[128,1024]{1,0:T(8,128)S(1)} %copy.46, f32[128,1024]{1,0:T(8,128)S(1)} %copy.45), kind=kLoop, calls=%fused_computation.11 | loop fusion | flops 29360128 | bytes 51904512 | tf_op jit(solution)/shard_map/sub | solution.py:85
  365.8 17.2 %fusion.3 = f32[2,16,128,1024]{3,2,1,0:T(8,128)} fusion(f32[2,16,128,1024]{3,2,1,0:T(8,128)} %param.12, f32[1,16,128,1024]{3,2,1,0:T(8,128)} %get-tuple-element.5, f32[1,16,128,1024]{3,2,1,0:T(8,128)} %get-tuple-element.4), kind=kLoop, calls=%fused_computation.7 | loop fusion | flops 12582912 | bytes 50331648 | tf_op jit(solution)/shard_map/add | solution.py:107
  383.1 6.2 %fusion.31 = f32[2,128,1024]{2,1,0:T(8,128)S(1)} fusion(f32[1024,1024,1]{1,0,2:T(8,128)} %constant.31, f32[2,2,128,1024]{3,2,0,1:T(8,128)} %all-gather.5.cloned.1.call-done), kind=kOutput, calls=%fused_computation.60 | convolution fusion | flops 3221225472 | bytes 6291456 | tf_op jit(solution)/shard_map/fmn,nk->fmk/dot_general | solution.py:56
  389.2 6.2 %fusion.30 = f32[2,128,1024]{2,1,0:T(8,128)S(1)} fusion(f32[1024,1024,1]{1,0,2:T(8,128)} %constant.31, f32[2,2,128,1024]{3,2,0,1:T(8,128)} %all-gather.5.cloned.1.call-done), kind=kOutput, calls=%fused_computation.59 | convolution fusion | flops 3221225472 | bytes 6291456 | tf_op jit(solution)/shard_map/fmn,nk->fmk/dot_general | solution.py:56
  (71 shorter events, 62.4 us)
Async XLA Ops:
  7.2 213.6 %copy-start = (f32[16]{0:T(128)S(1)}, f32[16]{0:T(128)}, u32[]{:S(2)}) copy-start(f32[16]{0:T(128)} %param.14) | copy-start | bytes 196
  7.2 7.9 %copy-start.5 = (f32[2,128,1024]{2,1,0:T(8,128)S(1)}, f32[2,128,1024]{2,1,0:T(8,128)}, u32[]{:S(2)}) copy-start(f32[2,128,1024]{2,1,0:T(8,128)} %param.10) | copy-start | bytes 3145732
  7.2 7.9 %copy-start.6 = (f32[2,128,1024]{2,1,0:T(8,128)S(1)}, f32[2,128,1024]{2,1,0:T(8,128)}, u32[]{:S(2)}) copy-start(f32[2,128,1024]{2,1,0:T(8,128)} %param.9) | copy-start | bytes 3145732
  7.2 103.8 %all-gather.3.cloned.1.call-start = ((), (), s32[]{:S(2)}) async-start(), calls=%async_computation.5 | async-start | bytes 2621440 | tf_op jit(solution)/shard_map/all_gather | solution.py:140
  39.8 12.7 %copy-start.1 = (f32[1024,1024,1]{1,0,2:T(8,128)S(1)}, f32[1024,1024,1]{1,0,2:T(8,128)}, u32[]{:S(2)}) copy-start(f32[1024,1024,1]{1,0,2:T(8,128)} %constant.32) | copy-start | bytes 12582916
  64.8 48.7 %copy-start.9 = (f32[128,1024]{1,0:T(8,128)S(1)}, f32[128,1024]{1,0:T(8,128)}, u32[]{:S(2)}) copy-start(f32[128,1024]{1,0:T(8,128)} %param.15) | copy-start | bytes 1572868
  89.2 179.1 %reduce-scatter.2.cloned.1.call-start = ((), (), s32[]{:S(2)}) async-start(), calls=%async_computation.6 | async-start | bytes 1310720 | tf_op jit(solution)/shard_map/reduce_scatter | solution.py:156
  113.5 18.6 %copy-start.10 = (f32[16]{0:T(128)S(1)}, f32[16]{0:T(128)}, u32[]{:S(2)}) copy-start(f32[16]{0:T(128)} %param.13) | copy-start | bytes 196
  214.6 6.2 %copy-start.4 = (f32[2,16,128,1024]{3,2,1,0:T(8,128)}, f32[2,16,128,1024]{3,2,1,0:T(8,128)S(1)}, u32[]{:S(2)}) copy-start(f32[2,16,128,1024]{3,2,1,0:T(8,128)S(1)} %fusion.2) | copy-start | bytes 50331652
  220.8 22.7 %copy-start.7 = (f32[2,2,128,1024]{2,3,1,0:T(8,128)S(1)}, f32[2,2,128,1024]{2,3,1,0:T(8,128)}, u32[]{:S(2)}) copy-start(f32[2,2,128,1024]{2,3,1,0:T(8,128)} %all-gather.3.cloned.1.call-done) | copy-start | bytes 6291460
  243.4 139.7 %all-gather.5.cloned.1.call-start = ((), (), s32[]{:S(2)}) async-start(), calls=%async_computation.7 | async-start | bytes 2621440 | tf_op jit(solution)/shard_map/all_gather | solution.py:140
  290.1 12.7 %copy-start.2 = (f32[1024,1024,1]{1,0,2:T(8,128)S(1)}, f32[1024,1024,1]{1,0,2:T(8,128)}, u32[]{:S(2)}) copy-start(f32[1024,1024,1]{1,0,2:T(8,128)} %constant.32) | copy-start | bytes 12582916
  383.1 12.4 %copy-start.3 = (f32[1024,1024,1]{1,0,2:T(8,128)S(1)}, f32[1024,1024,1]{1,0,2:T(8,128)}, u32[]{:S(2)}) copy-start(f32[1024,1024,1]{1,0,2:T(8,128)} %constant.32) | copy-start | bytes 12582916
  383.1 12.4 %copy-start.8 = (f32[2,2,128,1024]{3,2,0,1:T(8,128)S(1)}, f32[2,2,128,1024]{3,2,0,1:T(8,128)}, u32[]{:S(2)}) copy-start(f32[2,2,128,1024]{3,2,0,1:T(8,128)} %all-gather.5.cloned.1.call-done) | copy-start | bytes 6291460
Sparse Core Ops, SparseCore 0:
  89.3 21.6 all-gather.2
  243.5 24.8 reduce-scatter.1
  345.7 20.6 all-gather.4
where the time goes:
time: 416 us; the launch traced here: 411 us
  other arithmetic  149 us (36%)
  matrix products  89.2 us (21%)
  blocking collectives  76.7 us (18%)
  waiting for transfers between devices  45.6 us (11%)
  local copies, waits for them, and re-layouts  36 us (9%)
  between operations  14.3 us (3%)
    dot_general x8, matrix products, product_of(): return jnp.einsum('mn,fnk->fmk', table, values, precision=HIGHEST)  42.5 us
    all_to_all x2, blocking collectives, row_mix(): lax.all_to_all(section, 'space', split_axis=3, concat_axis=2, tiled=True)  41.3 us
    sub x2, other arithmetic, derivative(): -DEPHASE * spin_real + gradient * spin_imag  38.9 us
    sub x2, other arithmetic, derivative(): -GAMMA * optical_real + doppler * optical_imag - probe_imag  36.8 us
    all_to_all x2, blocking collectives, row_mix(): lax.all_to_all(blended, 'space', split_axis=2, concat_axis=3, tiled=True)  35.4 us
    add x1, other arithmetic, midpoint(): half_optical = optical + 0.5 * DT * rate_optical  33.9 us
    dot_general x8, matrix products, product_of(): return jnp.einsum('fmn,nk->fmk', values, table, precision=HIGHEST)  30 us
    add x2, other arithmetic, midpoint(): return (optical + DT * rate_optical, spin_part + DT * rate_spin)  29.1 us
  transfers between devices with their start and end apart: 3, of which 2 were waited for; matrix products, arithmetic and copies ran while one was open for 9% of the time, Pallas kernels for 0%

commit v1 on v0

--- a/solution.py
+++ b/solution.py
@@ -1,18 +1,17 @@
+import functools
 import jax
 import jax.numpy as jnp
 import numpy as np
 from jax import lax
+from jax.experimental import pallas as pl
+from jax.experimental.pallas import tpu as pltpu
 from jax.sharding import PartitionSpec as P
-
-GRID = 1024
-VEL = 64
-
 
 GAMMA = 1.0
 DEPHASE = 0.1
 DT = 0.25
 COUPLE = 2.0
-HIGHEST = lax.Precision.HIGHEST
+EXACT = lax.Precision.HIGH
 
 
 def circulant_tables(grid_width):
@@ -38,7 +37,7 @@
     real_in, imag_in = (section[:, 0], section[:, 1])
 
     def product_of(table, values):
-        return jnp.einsum("mn,fnk->fmk", table, values, precision=HIGHEST)
+        return jnp.einsum("mn,fnk->fmk", table, values, precision=EXACT)
 
     return jnp.stack(
         [
@@ -53,7 +52,7 @@
     real_in, imag_in = (section[:, 0], section[:, 1])
 
     def product_of(values, table):
-        return jnp.einsum("fmn,nk->fmk", values, table, precision=HIGHEST)
+        return jnp.einsum("fmn,nk->fmk", values, table, precision=EXACT)
 
     return jnp.stack(
         [
@@ -64,47 +63,88 @@
     )
 
 
-def derivative(optical, spin_part, probe_part, control, doppler, gradient):
-    optical_real, optical_imag = (optical[0], optical[1])
-    spin_real, spin_imag = (spin_part[0], spin_part[1])
-    probe_real, probe_imag = (probe_part[0], probe_part[1])
-    control_real, control_imag = (control[0], control[1])
-    rate_optical_real = (
-        -GAMMA * optical_real
-        + doppler * optical_imag
-        - probe_imag
-        - (control_real * spin_imag + control_imag * spin_real)
-    )
-    rate_optical_imag = (
-        -GAMMA * optical_imag
-        - doppler * optical_real
-        + probe_real
-        + (control_real * spin_real - control_imag * spin_imag)
-    )
-    rate_spin_real = (
-        -DEPHASE * spin_real
-        + gradient * spin_imag
-        - (control_real * optical_imag - control_imag * optical_real)
-    )
-    rate_spin_imag = (
-        -DEPHASE * spin_imag
-        - gradient * spin_real
-        + (control_real * optical_real + control_imag * optical_imag)
-    )
-    return (
-        jnp.stack([rate_optical_real, rate_optical_imag]),
-        jnp.stack([rate_spin_real, rate_spin_imag]),
-    )
-
-
-def midpoint(optical, spin_part, probe_part, control, doppler, gradient):
-    rate_optical, rate_spin = derivative(optical, spin_part, probe_part, control, doppler, gradient)
-    half_optical = optical + 0.5 * DT * rate_optical
-    half_spin = spin_part + 0.5 * DT * rate_spin
-    rate_optical, rate_spin = derivative(
-        half_optical, half_spin, probe_part, control, doppler, gradient
-    )
-    return (optical + DT * rate_optical, spin_part + DT * rate_spin)
+def state_kernel(doppler_ref, weight_ref, probe_ref, control_ref, gradient_ref, optical_ref, spin_ref, optical_out, spin_out, total_ref, *, scale):
+    classes = optical_ref.shape[1]
+    width = optical_ref.shape[3]
+    step = DT
+    half = 0.5 * DT * DT
+
+    def lane_block(block, carry):
+        lanes = pl.ds(pl.multiple_of(block * 128, 128), 128)
+        probe_real, probe_imag = probe_ref[0, :, lanes], probe_ref[1, :, lanes]
+        control_real, control_imag = control_ref[0, :, lanes], control_ref[1, :, lanes]
+        gradient = gradient_ref[:, lanes]
+        power = half * (control_real * control_real + control_imag * control_imag)
+        keep_real = step - half * (GAMMA + DEPHASE)
+        keep_imag = -half * gradient
+        into_real = -control_imag * keep_real - control_real * keep_imag
+        into_imag = control_real * keep_real - control_imag * keep_imag
+        back_real = control_imag * keep_real - control_real * keep_imag
+        back_imag = control_real * keep_real + control_imag * keep_imag
+        slope_real, slope_imag = half * control_real, half * control_imag
+        source_real = -(step - half * GAMMA) * probe_imag
+        source_imag = (step - half * GAMMA) * probe_real
+        drive_real, drive_imag = half * probe_real, half * probe_imag
+        spin_source_real = -half * (control_real * probe_real + control_imag * probe_imag)
+        spin_source_imag = -half * (control_real * probe_imag - control_imag * probe_real)
+        decay_real = 1.0 - step * DEPHASE + half * (DEPHASE * DEPHASE - gradient * gradient) - power
+        decay_imag = (2.0 * half * DEPHASE - step) * gradient
+        sum_real = jnp.zeros_like(gradient)
+        sum_imag = jnp.zeros_like(gradient)
+        for item in range(classes):
+            shift = doppler_ref[item]
+            weight = weight_ref[item] * scale
+            self_real = (1.0 - step * GAMMA + half * (GAMMA * GAMMA - shift * shift)) - power
+            self_imag = (2.0 * half * GAMMA - step) * shift
+            turn_real, turn_imag = shift * slope_real, shift * slope_imag
+            pull_real, pull_imag = into_real + turn_real, into_imag + turn_imag
+            push_real, push_imag = back_real + turn_real, back_imag - turn_imag
+            a_real, a_imag = optical_ref[0, item, :, lanes], optical_ref[1, item, :, lanes]
+            b_real, b_imag = spin_ref[0, item, :, lanes], spin_ref[1, item, :, lanes]
+            new_real = (
+                self_real * a_real - self_imag * a_imag + pull_real * b_real - pull_imag * b_imag
+                + (source_real + shift * drive_real)
+            )
+            new_imag = (
+                self_real * a_imag + self_imag * a_real + pull_real * b_imag + pull_imag * b_real
+                + (source_imag + shift * drive_imag)
+            )
+            optical_out[0, item, :, lanes] = new_real
+            optical_out[1, item, :, lanes] = new_imag
+            spin_out[0, item, :, lanes] = (
+                push_real * a_real - push_imag * a_imag + decay_real * b_real - decay_imag * b_imag + spin_source_real
+            )
+            spin_out[1, item, :, lanes] = (
+                push_real * a_imag + push_imag * a_real + decay_real * b_imag + decay_imag * b_real + spin_source_imag
+            )
+            sum_real += weight * new_real
+            sum_imag += weight * new_imag
+        total_ref[0, :, lanes] = sum_real
+        total_ref[1, :, lanes] = sum_imag
+        return carry
+
+    lax.fori_loop(0, width // 128, lane_block, 0)
+
+
+def advance(optical, spin_part, probe_part, control, doppler, weight, gradient, scale):
+    _, classes, rows, width = optical.shape
+    tall = 8
+    state = pl.BlockSpec((2, classes, tall, width), lambda i: (0, 0, i, 0))
+    plane = pl.BlockSpec((2, tall, width), lambda i: (0, i, 0))
+    small = pl.BlockSpec(memory_space=pltpu.SMEM)
+    return pl.pallas_call(
+        functools.partial(state_kernel, scale=scale),
+        grid=(rows // tall,),
+        in_specs=[small, small, plane, plane, pl.BlockSpec((tall, width), lambda i: (i, 0)), state, state],
+        out_specs=[state, state, plane],
+        out_shape=[
+            jax.ShapeDtypeStruct(optical.shape, jnp.float32),
+            jax.ShapeDtypeStruct(spin_part.shape, jnp.float32),
+            jax.ShapeDtypeStruct((2, rows, width), jnp.float32),
+        ],
+        compiler_params=pltpu.CompilerParams(vmem_limit_bytes=40 << 20),
+        name="advance_states",
+    )(doppler, weight, probe_part, control, gradient, optical, spin_part)
 
 
 def add_source(complex_field, polarization):
@@ -122,7 +162,7 @@
     class_weight,
     gradient_shift,
 ):
-    grid_width = GRID
+    grid_width = probe_field.shape[2]
     quarter_width = grid_width // lax.axis_size("vel")
     table_real, table_imag = circulant_tables(grid_width)
     full_real = jnp.asarray(table_real)
@@ -144,15 +184,16 @@
     quart_real = lax.dynamic_slice_in_dim(full_real, col_start, quarter_width, 1)
     quart_imag = lax.dynamic_slice_in_dim(full_imag, col_start, quarter_width, 1)
     stacked = spread(row_mix(mix_right(stacked, quart_real, quart_imag)))
-    optical_new, spin_new = midpoint(
+    optical_new, spin_new, weighted = advance(
         optical_state,
         spin_state,
         stacked[0],
         stacked[1],
-        doppler_shift[:, None, None],
+        doppler_shift,
+        class_weight,
         gradient_shift,
-    )
-    weighted = jnp.einsum("cvrn,v->crn", optical_new, class_weight, precision=HIGHEST) / VEL
+        1.0 / (optical_state.shape[1] * lax.axis_size("vel")),
+    )
     polarization = lax.psum_scatter(weighted, "vel", scatter_dimension=2, tiled=True)
     probe_part = lax.dynamic_slice_in_dim(stacked[0], col_start, quarter_width, 2)
     control_part = lax.dynamic_slice_in_dim(stacked[1], col_start, quarter_width, 2)

time: 416 us -> 265 us (0.64)
  other arithmetic: 149 us -> 6.41 us
  matrix products: 89.2 us -> 43.1 us
  Pallas kernels: 0 us -> 33.4 us
  waiting for transfers between devices: 45.6 us -> 67.5 us
  local copies, waits for them, and re-layouts: 36 us -> 19.3 us
    sub x4 -> x0, other arithmetic: 75.6 us -> none  [the longest x2 38.9 us: derivative(): -DEPHASE * spin_real + gradient * spin_imag]
    add x3 -> x0, other arithmetic: 63 us -> none  [the longest x1 33.9 us: midpoint(): half_optical = optical + 0.5 * DT * rate_optical]
    dot_general x17 -> x16, matrix products: 89.2 us -> 43.1 us  [the longest x8 25.9 us: product_of(): return jnp.einsum('mn,fnk->fmk', table, values, precision=EXACT)]
    pallas_call x0 -> x1, Pallas kernels: none -> 33.4 us  [advance(): pl.pallas_call(functools.partial(state_kernel, scale=scale), grid=(rows /...]
    all_gather x2, waiting for transfers between devices: 21.8 us -> 42.6 us  [spread(): return lax.all_gather(section, 'vel', axis=3, tiled=True)]
    unnamed x26, local copies, waits for them, and re-layouts: 15.7 us -> 7.65 us
  transfers between devices with their start and end apart: 3 -> 3, of which waited for: 2 -> 3; matrix products, arithmetic and copies ran while one was open for 9% -> 0% of each run, Pallas kernels for 0% -> 0%
where the time goes in v1:
time: 265 us; the launch traced here: 262 us
  blocking collectives  77 us (29%)
  waiting for transfers between devices  67.5 us (25%)
  matrix products  43.1 us (16%)
  Pallas kernels  33.4 us (13%)
  local copies, waits for them, and re-layouts  19.3 us (7%)
  between operations  14.6 us (6%)
  other arithmetic  6.41 us (2%)
    all_gather x2, waiting for transfers between devices, spread(): return lax.all_gather(section, 'vel', axis=3, tiled=True)  42.6 us
    all_to_all x2, blocking collectives, row_mix(): lax.all_to_all(section, 'space', split_axis=3, concat_axis=2, tiled=True)  41.5 us
    all_to_all x2, blocking collectives, row_mix(): lax.all_to_all(blended, 'space', split_axis=2, concat_axis=3, tiled=True)  35.5 us
    pallas_call x1, Pallas kernels, advance(): pl.pallas_call(functools.partial(state_kernel, scale=scale), grid=(rows /...  33.4 us
    dot_general x8, matrix products, product_of(): return jnp.einsum('mn,fnk->fmk', table, values, precision=EXACT)  25.9 us
    reduce_scatter x1, waiting for transfers between devices, shards(): lax.psum_scatter(weighted, 'vel', scatter_dimension=2, tiled=True)  24.9 us
    dot_general x8, matrix products, product_of(): return jnp.einsum('fmn,nk->fmk', values, table, precision=EXACT)  17.3 us
    unnamed x26, local copies, waits for them, and re-layouts  7.65 us
  transfers between devices with their start and end apart: 3, of which 3 were waited for; matrix products, arithmetic and copies ran while one was open for 0% of the time, Pallas kernels for 0%

profile of v1, /device:TPU:0, one launch (start us, length us, event | category | flops | bytes accessed | tf_op | source)
XLA Modules:
  0.0 261.6 jit_solution(5596505573583954164)
XLA Ops:
  7.3 2.3 fusion.18
  9.6 2.2 fusion.20
  13.5 21.8 %all_to_all.72 = f32[2,2,128,256]{2,0,1,3:T(2,128)S(1)} all-to-all(f32[2,2,128,256]{2,0,1,3:T(2,128)S(1)} %copy.35), channel_id=1, replica_groups=mesh['space'=8,'vel'=4] {'space'}, dimensions={3} | all-to-all | bytes 1048576 | tf_op jit(solution)/shard_map/all_to_all | solution.py:175
  35.7 4.4 %fusion.29 = f32[2,32,1024]{2,1,0:T(8,128)S(1)} fusion(f32[1024,1024,1]{1,0,2:T(8,128)} %constant.20, f32[2,2,1024,32]{2,3,0,1:T(8,128)S(1)} %all_to_all.55), kind=kOutput, calls=%fused_computation.52 | convolution fusion | flops 402653184 | bytes 4718592 | tf_op jit(solution)/shard_map/mn,fnk->fmk/dot_general | solution.py:40
  40.1 4.2 %fusion.28 = f32[2,32,1024]{2,1,0:T(8,128)S(1)} fusion(f32[1024,1024,1]{1,0,2:T(8,128)} %constant.20, f32[2,2,1024,32]{2,3,0,1:T(8,128)S(1)} %all_to_all.55), kind=kOutput, calls=%fused_computation.51 | convolution fusion | flops 402653184 | bytes 4718592 | tf_op jit(solution)/shard_map/mn,fnk->fmk/dot_general | solution.py:40
  44.3 2.2 fusion.4
  46.5 2.2 fusion.5
  50.1 2.0 reshape.21
  52.1 17.8 %all_to_all.73 = f32[8,1,16384]{2,1,0:T(1,128)S(1)} all-to-all(f32[8,1,16384]{2,1,0:T(1,128)S(1)} %reshape.21), channel_id=1, replica_groups=mesh['space'=8,'vel'=4] {'space'}, dimensions={0} | all-to-all | bytes 1048576 | tf_op jit(solution)/shard_map/all_to_all | solution.py:177
  76.6 21.8 %all-gather.3.cloned.1.call-done = f32[2,2,128,1024]{3,2,1,0:T(8,128)} async-done(((f32[2,2,128,256]{3,2,1,0:T(8,128)}), f32[2,2,128,1024]{3,2,1,0:T(8,128)}) %all-gather.3.cloned.1.call-update) | async-done | bytes 2097168 | tf_op jit(solution)/shard_map/all_gather | solution.py:180
  98.4 2.1 fusion.44
  100.5 33.4 %advance_states.1 = (f32[2,16,128,1024]{3,2,1,0:T(8,128)}, f32[2,16,128,1024]{3,2,1,0:T(8,128)}, f32[2,128,1024]{2,1,0:T(8,128)}) custom-call(f32[16]{0:T(128)S(1)} %copy-done.1, f32[16]{0:T(128)S(1)} %copy-done.2, f32[2,128,1024]{2,1,0:T(8,128)S(1)} %get-tuple-element.13.probe_ref, f32[2,128,1024]{2,1,0:T(8,128)S(1)} %get-tuple-element.14.control_ref, ...), custom_call_target="tpu_custom_call" | custom-call | tf_op jit(solution)/shard_map/advance_states/pallas_call | solution.py:135
  134.0 24.9 %reduce-scatter.2.cloned.1.call-done = f32[2,128,256]{2,1,0:T(8,128)} async-done(((f32[2,128,1024]{2,1,0:T(8,128)}), f32[2,128,256]{2,1,0:T(8,128)}) %reduce-scatter.2.cloned.1.call-update) | async-done | bytes 262160 | tf_op jit(solution)/shard_map/reduce_scatter | solution.py:197
  160.2 19.7 %all_to_all.74 = f32[2,2,128,256]{2,1,0,3:T(2,128)S(1)} all-to-all(f32[2,2,128,256]{2,1,0,3:T(2,128)S(1)} %copy.42), channel_id=1, replica_groups=mesh['space'=8,'vel'=4] {'space'}, dimensions={3} | all-to-all | bytes 1048576 | tf_op jit(solution)/shard_map/all_to_all | solution.py:175
  180.4 4.4 %fusion.31 = f32[2,32,1024]{2,1,0:T(8,128)S(1)} fusion(f32[1024,1024,1]{1,0,2:T(8,128)} %constant.20, f32[2,2,1024,32]{2,3,0,1:T(8,128)S(1)} %all_to_all.63), kind=kOutput, calls=%fused_computation.54 | convolution fusion | flops 402653184 | bytes 4718592 | tf_op jit(solution)/shard_map/mn,fnk->fmk/dot_general | solution.py:40
  184.8 4.2 %fusion.30 = f32[2,32,1024]{2,1,0:T(8,128)S(1)} fusion(f32[1024,1024,1]{1,0,2:T(8,128)} %constant.20, f32[2,2,1024,32]{2,3,0,1:T(8,128)S(1)} %all_to_all.63), kind=kOutput, calls=%fused_computation.53 | convolution fusion | flops 402653184 | bytes 4718592 | tf_op jit(solution)/shard_map/mn,fnk->fmk/dot_general | solution.py:40
  189.0 2.2 fusion.2
  191.1 2.2 fusion.3
  196.8 17.8 %all_to_all.75 = f32[8,1,16384]{2,1,0:T(1,128)S(1)} all-to-all(f32[8,1,16384]{2,1,0:T(1,128)S(1)} %reshape.23), channel_id=1, replica_groups=mesh['space'=8,'vel'=4] {'space'}, dimensions={0} | all-to-all | bytes 1048576 | tf_op jit(solution)/shard_map/all_to_all | solution.py:177
  220.7 20.9 %all-gather.5.cloned.1.call-done = f32[2,2,128,1024]{3,2,0,1:T(8,128)} async-done(((f32[2,2,128,256]{3,2,0,1:T(8,128)}), f32[2,2,128,1024]{3,2,0,1:T(8,128)}) %all-gather.5.cloned.1.call-update) | async-done | bytes 2097168 | tf_op jit(solution)/shard_map/all_gather | solution.py:180
  241.5 4.7 %fusion.25 = f32[2,128,1024]{2,1,0:T(8,128)S(1)} fusion(f32[1024,1024,1]{1,0,2:T(8,128)} %constant.20, f32[2,2,128,1024]{3,2,0,1:T(8,128)} %all-gather.5.cloned.1.call-done), kind=kOutput, calls=%fused_computation.41 | convolution fusion | flops 1610612736 | bytes 6291456 | tf_op jit(solution)/shard_map/fmn,nk->fmk/dot_general | solution.py:55
  246.3 2.3 fusion.24
  248.6 2.3 fusion
  250.8 2.3 fusion.1
  (58 shorter events, 23.1 us)
Async XLA Ops:
  7.2 4.6 %copy-start.7 = (f32[2,128,1024]{2,1,0:T(8,128)S(1)}, f32[2,128,1024]{2,1,0:T(8,128)}, u32[]{:S(2)}) copy-start(f32[2,128,1024]{2,1,0:T(8,128)} %param.10) | copy-start | bytes 3145732
  7.2 4.6 %copy-start.8 = (f32[2,128,1024]{2,1,0:T(8,128)S(1)}, f32[2,128,1024]{2,1,0:T(8,128)}, u32[]{:S(2)}) copy-start(f32[2,128,1024]{2,1,0:T(8,128)} %param.9) | copy-start | bytes 3145732
  7.2 91.2 %all-gather.3.cloned.1.call-start = ((), (), s32[]{:S(2)}) async-start(), calls=%async_computation.5 | async-start | bytes 2621440 | tf_op jit(solution)/shard_map/all_gather | solution.py:180
  7.2 4.6 %copy-start.10 = (f32[1024,1024]{1,0:T(8,128)S(1)}, f32[1024,1024]{1,0:T(8,128)}, u32[]{:S(2)}) copy-start(f32[1024,1024]{1,0:T(8,128)} %constant.19.clone) | copy-start | bytes 12582916
  35.7 8.6 %copy-start.3 = (f32[1024,1024,1]{1,0,2:T(8,128)S(1)}, f32[1024,1024,1]{1,0,2:T(8,128)}, u32[]{:S(2)}) copy-start(f32[1024,1024,1]{1,0,2:T(8,128)} %constant.21) | copy-start | bytes 12582916
  75.5 24.9 %copy-start = (f32[128,1024]{1,0:T(8,128)S(1)}, f32[128,1024]{1,0:T(8,128)}, u32[]{:S(2)}) copy-start(f32[128,1024]{1,0:T(8,128)} %gradient_ref.1) | copy-start | bytes 1572868
  75.5 24.9 %copy-start.1 = (f32[16]{0:T(128)S(1)}, f32[16]{0:T(128)}, u32[]{:S(2)}) copy-start(f32[16]{0:T(128)} %doppler_ref.1) | copy-start | bytes 196
  75.6 24.9 %copy-start.2 = (f32[16]{0:T(128)S(1)}, f32[16]{0:T(128)}, u32[]{:S(2)}) copy-start(f32[16]{0:T(128)} %weight_ref.1) | copy-start | bytes 196
  76.6 82.2 %reduce-scatter.2.cloned.1.call-start = ((), (), s32[]{:S(2)}) async-start(), calls=%async_computation.6 | async-start | bytes 1310720 | tf_op jit(solution)/shard_map/reduce_scatter | solution.py:197
  133.9 107.6 %all-gather.5.cloned.1.call-start = ((), (), s32[]{:S(2)}) async-start(), calls=%async_computation.7 | async-start | bytes 2621440 | tf_op jit(solution)/shard_map/all_gather | solution.py:180
  180.4 8.6 %copy-start.4 = (f32[1024,1024,1]{1,0,2:T(8,128)S(1)}, f32[1024,1024,1]{1,0,2:T(8,128)}, u32[]{:S(2)}) copy-start(f32[1024,1024,1]{1,0,2:T(8,128)} %constant.21) | copy-start | bytes 12582916
  241.5 4.7 %copy-start.6 = (f32[1024,1024,1]{1,0,2:T(8,128)S(1)}, f32[1024,1024,1]{1,0,2:T(8,128)}, u32[]{:S(2)}) copy-start(f32[1024,1024,1]{1,0,2:T(8,128)} %constant.20) | copy-start | bytes 12582916
  241.5 4.7 %copy-start.9 = (f32[2,2,128,1024]{3,2,0,1:T(8,128)S(1)}, f32[2,2,128,1024]{3,2,0,1:T(8,128)}, u32[]{:S(2)}) copy-start(f32[2,2,128,1024]{3,2,0,1:T(8,128)} %all-gather.5.cloned.1.call-done) | copy-start | bytes 6291460
  246.3 2.3 copy-start.5
Sparse Core Ops, SparseCore 0:
  76.7 21.6 all-gather.2
  134.0 24.7 reduce-scatter.1
  220.8 20.6 all-gather.4

commit v2 on v1

--- a/solution.py
+++ b/solution.py
@@ -11,56 +11,268 @@
 DEPHASE = 0.1
 DT = 0.25
 COUPLE = 2.0
-EXACT = lax.Precision.HIGH
-
-
-def circulant_tables(grid_width):
-    counter = np.arange(grid_width, dtype=np.int32)
-    frequency = np.where(counter < grid_width // 2, counter, counter - grid_width)
-    angles = (
-        np.float32(np.pi)
-        * (frequency * frequency % (2 * grid_width)).astype(np.float32)
-        / np.float32(grid_width)
-    )
-    turns = counter[:, None] * counter[None, :] % grid_width
-    argument = (
-        np.float32(2.0 * np.pi) * turns.astype(np.float32) / np.float32(grid_width)
-        - angles[None, :]
-    )
-    kernel_real = np.mean(np.cos(argument), axis=1)
-    kernel_imag = np.mean(np.sin(argument), axis=1)
-    offsets = (counter[:, None] - counter[None, :]) % grid_width
-    return (kernel_real[offsets].astype(np.float32), kernel_imag[offsets].astype(np.float32))
-
-
-def mix_left(table_real, table_imag, section):
-    real_in, imag_in = (section[:, 0], section[:, 1])
-
-    def product_of(table, values):
-        return jnp.einsum("mn,fnk->fmk", table, values, precision=EXACT)
-
-    return jnp.stack(
-        [
-            product_of(table_real, real_in) - product_of(table_imag, imag_in),
-            product_of(table_real, imag_in) + product_of(table_imag, real_in),
-        ],
-        axis=1,
-    )
-
-
-def mix_right(section, table_real, table_imag):
-    real_in, imag_in = (section[:, 0], section[:, 1])
-
-    def product_of(values, table):
-        return jnp.einsum("fmn,nk->fmk", values, table, precision=EXACT)
-
-    return jnp.stack(
-        [
-            product_of(real_in, table_real) - product_of(imag_in, table_imag),
-            product_of(imag_in, table_real) + product_of(real_in, table_imag),
-        ],
-        axis=1,
-    )
+BAND = 128
+MESH = pl.DeviceIdType.MESH
+
+
+def mixing_tables(width):
+    counter = np.arange(width)
+    frequency = np.where(counter < width // 2, counter, counter - width)
+    angles = np.pi * (frequency * frequency % (2 * width)) / width
+    kernel = np.fft.ifft(np.exp(-1j * angles))
+    band = kernel[(np.arange(BAND)[:, None] - np.arange(2 * width)[None, :]) % width]
+    full = np.stack([band.real, band.imag]).astype(np.float32)
+    high = full.astype(jnp.bfloat16)
+    low = (full - high.astype(np.float32)).astype(jnp.bfloat16)
+    return jnp.asarray(np.stack([high, low], axis=1))
+
+
+def split(values):
+    high = values.astype(jnp.bfloat16)
+    return high, (values - high.astype(jnp.float32)).astype(jnp.bfloat16)
+
+
+def outer_dot(left, right):
+    return lax.dot_general(left, right, (((1,), (1,)), ((), ())), preferred_element_type=jnp.float32)
+
+
+def inner_dot(left, right):
+    return jnp.dot(left, right, preferred_element_type=jnp.float32)
+
+
+class Mixer:
+    def __init__(self, spaces, groups, width, rows, table, scratch):
+        self.spaces, self.groups, self.width, self.rows = spaces, groups, width, rows
+        self.table = table
+        (self.high, self.low, self.out_chunks, self.in_chunks, self.back_chunks, self.gathered,
+         self.row_send, self.row_recv, self.back_send, self.back_recv,
+         self.far_send, self.far_recv, self.core_send, self.core_recv) = scratch
+        self.columns = width // groups
+        self.piece = self.columns // spaces
+        self.space = lax.axis_index("space")
+        self.vel = lax.axis_index("vel")
+        self.core = self.vel % 2
+        self.far = self.vel // 2
+        self.core_peer = self.far * 2 + 1 - self.core
+        self.sent = []
+
+    def far_peer(self, hop):
+        return ((self.far + hop) % (self.groups // 2)) * 2 + self.core
+
+    def enter(self):
+        barrier = pltpu.get_barrier_semaphore()
+        for hop in range(1, self.spaces):
+            pl.semaphore_signal(barrier, inc=1, device_id={"space": (self.space + hop) % self.spaces}, device_id_type=MESH)
+        for hop in range(1, self.groups // 2):
+            pl.semaphore_signal(barrier, inc=1, device_id={"vel": self.far_peer(hop)}, device_id_type=MESH)
+        pl.semaphore_signal(barrier, inc=1, device_id={"vel": self.core_peer}, device_id_type=MESH)
+        pl.semaphore_wait(barrier, self.spaces - 1 + self.groups // 2)
+
+    def push(self, source, target, send_sem, recv_sem, device):
+        copy = pltpu.make_async_remote_copy(
+            src_ref=source, dst_ref=target, send_sem=send_sem, recv_sem=recv_sem,
+            device_id=device, device_id_type=MESH,
+        )
+        copy.start()
+        self.sent.append(copy)
+        return copy
+
+    def columns_stage(self, field, real, imag):
+        rows, piece, spaces = self.rows, self.piece, self.spaces
+        for part, plane in enumerate((real, imag)):
+            high, low = split(plane)
+            self.high[part * rows:(part + 1) * rows, :] = high
+            self.low[part * rows:(part + 1) * rows, :] = low
+        products = []
+        for part in range(2):
+            bands = [[], []]
+            for block in range(self.columns // BAND):
+                start = self.width - self.vel * self.columns - block * BAND
+                lanes = pl.ds(pl.multiple_of(start, BAND), self.width)
+                for level in range(2):
+                    bands[level].append(self.table[part, level, :, lanes])
+            first = jnp.concatenate(bands[0], axis=0)
+            both = outer_dot(jnp.concatenate(bands[0] + bands[1], axis=0), self.high[...])
+            products.append(both[:self.columns] + both[self.columns:] + outer_dot(first, self.low[...]))
+        mixed = (
+            products[0][:, :rows] - products[1][:, rows:],
+            products[0][:, rows:] + products[1][:, :rows],
+        )
+        for target in range(spaces):
+            for part in range(2):
+                self.out_chunks[field, target, part * piece:(part + 1) * piece, :] = mixed[part][target * piece:(target + 1) * piece]
+        self.rows_in = getattr(self, "rows_in", {})
+        self.rows_in[field] = []
+        for hop in range(1, spaces):
+            target = (self.space + hop) % spaces
+            self.rows_in[field].append(self.push(
+                self.out_chunks.at[field, target], self.in_chunks.at[field, self.space],
+                self.row_send.at[field, hop], self.row_recv.at[field, hop], {"space": target},
+            ))
+        self.in_chunks[field, self.space] = self.out_chunks[field, self.space]
+
+    def rows_stage(self, field):
+        rows, piece, spaces, width = self.rows, self.piece, self.spaces, self.width
+        for copy in self.rows_in[field]:
+            copy.wait_recv()
+        values = jnp.concatenate([self.in_chunks[field, source] for source in range(spaces)], axis=1)
+        high, low = split(values)
+        stacked = jnp.concatenate([high, low], axis=0)
+        tile = 2 * BAND
+        for start in range(0, width, tile):
+            products = []
+            for part in range(2):
+                bands = [
+                    jnp.concatenate([
+                        self.table[part, level, :, width - block * BAND + start:width - block * BAND + start + tile]
+                        if width - block * BAND + start + tile <= 2 * width
+                        else self.table[part, level, :, start - block * BAND:start - block * BAND + tile]
+                        for block in range(width // BAND)
+                    ], axis=0)
+                    for level in range(2)
+                ]
+                both = inner_dot(stacked, bands[0])
+                products.append(both[:2 * piece] + both[2 * piece:] + inner_dot(high, bands[1]))
+            real = products[0][:piece] - products[1][piece:]
+            imag = products[0][piece:] + products[1][:piece]
+            for offset in range(0, tile, rows):
+                target = (start + offset) // rows
+                self.back_chunks[field, target, :piece, :] = real[:, offset:offset + rows]
+                self.back_chunks[field, target, piece:, :] = imag[:, offset:offset + rows]
+        self.back_in = getattr(self, "back_in", {})
+        self.back_in[field] = []
+        for hop in range(1, spaces):
+            target = (self.space + hop) % spaces
+            self.back_in[field].append(self.push(
+                self.back_chunks.at[field, target], self.gathered.at[field, self.vel, self.space],
+                self.back_send.at[field, hop], self.back_recv.at[field, hop], {"space": target},
+            ))
+        self.gathered[field, self.vel, self.space] = self.back_chunks[field, self.space]
+
+    def spread_stage(self, field):
+        arrivals, core_copies = [], []
+        for hop in range(self.spaces):
+            source = (self.space + self.spaces - hop) % self.spaces
+            if hop:
+                self.back_in[field][hop - 1].wait_recv()
+            chunk = self.gathered.at[field, self.vel, source]
+            for far in range(1, self.groups // 2):
+                arrivals.append((far, hop, self.push(
+                    chunk, chunk, self.far_send.at[field, far, hop], self.far_recv.at[field, far, hop],
+                    {"vel": self.far_peer(far)},
+                )))
+            core_copies.append(self.push(
+                chunk, chunk, self.core_send.at[field, 0, hop], self.core_recv.at[field, 0, hop],
+                {"vel": self.core_peer},
+            ))
+        for far, hop, copy in arrivals:
+            copy.wait_recv()
+            source = (self.space + self.spaces - hop) % self.spaces
+            origin = self.far_peer(self.groups // 2 - far)
+            chunk = self.gathered.at[field, origin, source]
+            core_copies.append(self.push(
+                chunk, chunk, self.core_send.at[field, far, hop], self.core_recv.at[field, far, hop],
+                {"vel": self.core_peer},
+            ))
+        for copy in core_copies:
+            copy.wait_recv()
+
+    def finish(self, field, out_ref):
+        piece = self.piece
+        for start in range(0, self.width, BAND):
+            group = start // self.columns
+            first = (start % self.columns) // piece
+            for part in range(2):
+                block = jnp.concatenate([
+                    self.gathered[field, group, source, part * piece:(part + 1) * piece, :]
+                    for source in range(first, first + BAND // piece)
+                ], axis=0)
+                out_ref[part, :, start:start + BAND] = block.T
+
+    def leave(self):
+        for copy in self.sent:
+            copy.wait_send()
+
+
+def first_kernel(spaces, groups, probe_ref, control_ref, table_ref, probe_out, control_out, *scratch):
+    _, rows, width = probe_ref.shape
+    mixer = Mixer(spaces, groups, width, rows, table_ref, scratch)
+    mixer.enter()
+    mixer.columns_stage(0, probe_ref[0], probe_ref[1])
+    mixer.columns_stage(1, control_ref[0], control_ref[1])
+    mixer.rows_stage(0)
+    mixer.rows_stage(1)
+    mixer.spread_stage(0)
+    mixer.finish(0, probe_out)
+    mixer.spread_stage(1)
+    mixer.finish(1, control_out)
+    mixer.leave()
+
+
+def second_kernel(spaces, groups, probe_ref, control_ref, part_ref, table_ref, probe_out, control_out,
+                  core_part, far_parts, pair_sum, total, sum_send, sum_recv, *scratch):
+    _, rows, width = probe_ref.shape
+    mixer = Mixer(spaces, groups, width, rows, table_ref, scratch)
+    core, peer = mixer.core, {"vel": mixer.core_peer}
+    mixer.enter()
+    swap = mixer.push(part_ref.at[1 - core], core_part, sum_send.at[0], sum_recv.at[0], peer)
+    mixer.columns_stage(0, control_ref[0], control_ref[1])
+    swap.wait_recv()
+    pair_sum[...] = part_ref[core] + core_part[...]
+    swaps = [
+        mixer.push(pair_sum, far_parts.at[far], sum_send.at[1 + far], sum_recv.at[1 + far], {"vel": mixer.far_peer(far)})
+        for far in range(1, groups // 2)
+    ]
+    mixer.rows_stage(0)
+    whole = pair_sum[...]
+    for far, copy in enumerate(swaps, 1):
+        copy.wait_recv()
+        whole = whole + far_parts[far]
+    total[core] = whole
+    swap = mixer.push(total.at[core], total.at[core], sum_send.at[1], sum_recv.at[1], peer)
+    swap.wait_recv()
+    mixer.columns_stage(1, probe_ref[0] - COUPLE * total[1], probe_ref[1] + COUPLE * total[0])
+    mixer.spread_stage(0)
+    mixer.rows_stage(1)
+    mixer.finish(0, control_out)
+    mixer.spread_stage(1)
+    mixer.finish(1, probe_out)
+    mixer.leave()
+
+
+def diffract(kernel, spaces, groups, collective, fields, extra, table):
+    _, rows, width = fields[0].shape
+    piece = width // groups // spaces
+    chunks = pltpu.VMEM((2, spaces, 2 * piece, rows), jnp.float32)
+    dma = pltpu.SemaphoreType.DMA
+    scratch = [
+        pltpu.VMEM((2 * rows, width), jnp.bfloat16),
+        pltpu.VMEM((2 * rows, width), jnp.bfloat16),
+        chunks, chunks, chunks,
+        pltpu.VMEM((2, groups, spaces, 2 * piece, rows), jnp.float32),
+        dma((2, spaces)), dma((2, spaces)), dma((2, spaces)), dma((2, spaces)),
+        dma((2, groups // 2, spaces)), dma((2, groups // 2, spaces)),
+        dma((2, groups // 2, spaces)), dma((2, groups // 2, spaces)),
+    ]
+    if extra:
+        plane = pltpu.VMEM((rows, width), jnp.float32)
+        scratch = [
+            plane, pltpu.VMEM((groups // 2, rows, width), jnp.float32), plane,
+            pltpu.VMEM((2, rows, width), jnp.float32),
+            dma((1 + groups // 2,)), dma((1 + groups // 2,)),
+        ] + scratch
+    operands = (*fields, *extra, table)
+    vmem = pl.BlockSpec(memory_space=pltpu.VMEM)
+    shape = jax.ShapeDtypeStruct(fields[0].shape, jnp.float32)
+    return pl.pallas_call(
+        functools.partial(kernel, spaces, groups),
+        in_specs=[vmem] * len(operands),
+        out_specs=[vmem, vmem],
+        out_shape=[shape, shape],
+        scratch_shapes=scratch,
+        compiler_params=pltpu.CompilerParams(collective_id=collective, has_side_effects=True, vmem_limit_bytes=56 << 20),
+        name=kernel.__name__,
+    )(*operands)
 
 
 def state_kernel(doppler_ref, weight_ref, probe_ref, control_ref, gradient_ref, optical_ref, spin_ref, optical_out, spin_out, total_ref, *, scale):
@@ -147,13 +359,9 @@
     )(doppler, weight, probe_part, control, gradient, optical, spin_part)
 
 
-def add_source(complex_field, polarization):
-    return jnp.stack(
-        [complex_field[0] - COUPLE * polarization[1], complex_field[1] + COUPLE * polarization[0]]
-    )
-
-
 def shards(
+    spaces,
+    groups,
     probe_field,
     control_field,
     optical_state,
@@ -162,49 +370,25 @@
     class_weight,
     gradient_shift,
 ):
-    grid_width = probe_field.shape[2]
-    quarter_width = grid_width // lax.axis_size("vel")
-    table_real, table_imag = circulant_tables(grid_width)
-    full_real = jnp.asarray(table_real)
-    full_imag = jnp.asarray(table_imag)
-
-    def row_mix(section):
-        blended = mix_left(
-            full_real,
-            full_imag,
-            lax.all_to_all(section, "space", split_axis=3, concat_axis=2, tiled=True),
-        )
-        return lax.all_to_all(blended, "space", split_axis=2, concat_axis=3, tiled=True)
-
-    def spread(section):
-        return lax.all_gather(section, "vel", axis=3, tiled=True)
-
-    stacked = jnp.stack([probe_field, control_field])
-    col_start = lax.axis_index("vel") * quarter_width
-    quart_real = lax.dynamic_slice_in_dim(full_real, col_start, quarter_width, 1)
-    quart_imag = lax.dynamic_slice_in_dim(full_imag, col_start, quarter_width, 1)
-    stacked = spread(row_mix(mix_right(stacked, quart_real, quart_imag)))
+    table = mixing_tables(probe_field.shape[2])
+    probe_one, control_one = diffract(first_kernel, spaces, groups, 0, (probe_field, control_field), (), table)
     optical_new, spin_new, weighted = advance(
         optical_state,
         spin_state,
-        stacked[0],
-        stacked[1],
+        probe_one,
+        control_one,
         doppler_shift,
         class_weight,
         gradient_shift,
-        1.0 / (optical_state.shape[1] * lax.axis_size("vel")),
+        1.0 / (optical_state.shape[1] * groups),
     )
-    polarization = lax.psum_scatter(weighted, "vel", scatter_dimension=2, tiled=True)
-    probe_part = lax.dynamic_slice_in_dim(stacked[0], col_start, quarter_width, 2)
-    control_part = lax.dynamic_slice_in_dim(stacked[1], col_start, quarter_width, 2)
-    section = jnp.stack([add_source(probe_part, polarization), control_part])
-    stacked = mix_right(spread(row_mix(section)), full_real, full_imag)
-    return (stacked[0], stacked[1], optical_new, spin_new)
+    probe_out, control_out = diffract(second_kernel, spaces, groups, 1, (probe_one, control_one), (weighted,), table)
+    return (probe_out, control_out, optical_new, spin_new)
 
 
 def solution(mesh):
     return jax.shard_map(
-        shards,
+        functools.partial(shards, mesh.shape["space"], mesh.shape["vel"]),
         mesh=mesh,
         in_specs=(
             P(None, "space", None),

time: 265 us -> 141 us (0.53)
  Pallas kernels: 33.4 us -> 129 us
  blocking collectives: 77 us -> 0 us
  waiting for transfers between devices: 67.5 us -> 0 us
  matrix products: 43.1 us -> 0 us
  between operations: 14.6 us -> 0.66 us
  local copies, waits for them, and re-layouts: 19.3 us -> 10.4 us
  other arithmetic: 6.41 us -> 0 us
    pallas_call x0 -> x2, Pallas kernels: none -> 95.9 us  [diffract(): pl.pallas_call(functools.partial(kernel, spaces, groups), in_specs=[vmem]...]
    all_to_all x4 -> x0, blocking collectives: 77 us -> none  [the longest x2 41.5 us: row_mix(): lax.all_to_all(section, 'space', split_axis=3, concat_axis=2, tiled=True)]
    dot_general x16 -> x0, matrix products: 43.1 us -> none  [the longest x8 25.9 us: product_of(): return jnp.einsum('mn,fnk->fmk', table, values, precision=EXACT)]
    all_gather x2 -> x0, waiting for transfers between devices: 42.6 us -> none  [spread(): return lax.all_gather(section, 'vel', axis=3, tiled=True)]
    reduce_scatter x1 -> x0, waiting for transfers between devices: 24.9 us -> none  [shards(): lax.psum_scatter(weighted, 'vel', scatter_dimension=2, tiled=True)]
    all_to_all x11 -> x0, local copies, waits for them, and re-layouts: 6.25 us -> none  [the longest x5 5.39 us: row_mix(): lax.all_to_all(blended, 'space', split_axis=2, concat_axis=3, tiled=True)]
    all_to_all x2 -> x0, other arithmetic: 3.77 us -> none  [row_mix(): lax.all_to_all(blended, 'space', split_axis=2, concat_axis=3, tiled=True)]
    another operation x4 -> x0, local copies, waits for them, and re-layouts: 3.35 us -> none  [the longest x2 2.73 us: mix_left(): jnp.stack([product_of(table_real, real_in) - product_of(table_imag, imag_...]
  transfers between devices with their start and end apart: 3 -> 0, of which waited for: 3 -> 0; matrix products, arithmetic and copies ran while one was open for 0% -> 0% of each run, Pallas kernels for 0% -> 0%
where the time goes in v2:
time: 141 us; the launch traced here: 140 us
  Pallas kernels  129 us (91%)
  local copies, waits for them, and re-layouts  10.4 us (7%)
    pallas_call x2, Pallas kernels, diffract(): pl.pallas_call(functools.partial(kernel, spaces, groups), in_specs=[vmem]...  95.9 us
    pallas_call x1, Pallas kernels, advance(): pl.pallas_call(functools.partial(state_kernel, scale=scale), grid=(rows /...  33 us
    unnamed x14, local copies, waits for them, and re-layouts  10.4 us

profile of v2, /device:TPU:0, one launch (start us, length us, event | category | flops | bytes accessed | tf_op | source)
XLA Modules:
  0.0 140.0 jit_solution(17826405909007288290)
XLA Ops:
  0.6 45.0 %first_kernel.1 = (f32[2,128,1024]{2,1,0:T(8,128)}, f32[2,128,1024]{2,1,0:T(8,128)}) custom-call(f32[2,128,1024]{2,1,0:T(8,128)} %probe_ref.1, f32[2,128,1024]{2,1,0:T(8,128)} %control_ref.1, bf16[2,2,128,2048]{3,2,1,0:T(8,128)(2,1)} %constant.2.clone.table_ref), custom_call_target="tpu_custom_call" | custom-call | tf_op jit(solution)/shard_map/first_kernel/pallas_call | solution.py:267
  45.6 0.0 copy-start
  45.6 1.2 copy-done
  46.8 0.0 copy-start.1
  46.8 1.2 copy-done.1
  48.1 0.0 copy-start.3
  48.1 1.0 copy-done.3
  49.1 0.0 copy-start.4
  49.1 0.7 copy-done.4
  49.8 0.0 copy-start.5
  49.8 0.7 copy-done.5
  50.4 33.0 %advance_states.1 = (f32[2,16,128,1024]{3,2,1,0:T(8,128)}, f32[2,16,128,1024]{3,2,1,0:T(8,128)}, f32[2,128,1024]{2,1,0:T(8,128)S(1)}) custom-call(f32[16]{0:T(128)S(1)} %copy-done.4, f32[16]{0:T(128)S(1)} %copy-done.5, f32[2,128,1024]{2,1,0:T(8,128)S(1)} %copy-done, f32[2,128,1024]{2,1,0:T(8,128)S(1)} %copy-done.1, f32[128,1024]{1,0:T(8,128)S(1)} %copy-done.3, ...), custom_call_target="tpu_custom_call" | custom-call | tf_op jit(solution)/shard_map/advance_states/pallas_call | solution.py:347
  83.5 0.0 copy-start.2
  83.5 1.0 copy-done.2
  84.4 50.9 %second_kernel.1 = (f32[2,128,1024]{2,1,0:T(8,128)}, f32[2,128,1024]{2,1,0:T(8,128)}) custom-call(f32[2,128,1024]{2,1,0:T(8,128)} %get-tuple-element.11.probe_ref, f32[2,128,1024]{2,1,0:T(8,128)} %get-tuple-element.12.control_ref, f32[2,128,1024]{2,1,0:T(8,128)} %copy-done.2, bf16[2,2,128,2048]{3,2,1,0:T(8,128)(2,1)} %constant.2.clone.table_ref), custom_call_target="tpu_custom_call" | custom-call | tf_op jit(solution)/shard_map/second_kernel/pallas_call | solution.py:267
  135.4 2.3 %copy.14 = f32[2,128,1024]{2,1,0:T(8,128)} copy(f32[2,128,1024]{2,1,0:T(8,128)} %get-tuple-element.22) | data formatting | bytes 2097152
  137.7 2.3 %copy.15 = f32[2,128,1024]{2,1,0:T(8,128)} copy(f32[2,128,1024]{2,1,0:T(8,128)} %get-tuple-element.23) | data formatting | bytes 2097152
Async XLA Ops:
  45.6 1.2 copy-start
  46.8 1.2 copy-start.1
  48.1 1.0 copy-start.3
  49.1 0.7 copy-start.4
  49.8 0.7 copy-start.5
  83.5 1.0 copy-start.2

commit v3 on v2

--- a/solution.py
+++ b/solution.py
@@ -77,8 +77,8 @@
         self.sent.append(copy)
         return copy
 
-    def columns_stage(self, field, real, imag):
-        rows, piece, spaces = self.rows, self.piece, self.spaces
+    def columns_mix(self, vel, real, imag):
+        rows = self.rows
         for part, plane in enumerate((real, imag)):
             high, low = split(plane)
             self.high[part * rows:(part + 1) * rows, :] = high
@@ -87,17 +87,20 @@
         for part in range(2):
             bands = [[], []]
             for block in range(self.columns // BAND):
-                start = self.width - self.vel * self.columns - block * BAND
+                start = self.width - vel * self.columns - block * BAND
                 lanes = pl.ds(pl.multiple_of(start, BAND), self.width)
                 for level in range(2):
                     bands[level].append(self.table[part, level, :, lanes])
             first = jnp.concatenate(bands[0], axis=0)
             both = outer_dot(jnp.concatenate(bands[0] + bands[1], axis=0), self.high[...])
             products.append(both[:self.columns] + both[self.columns:] + outer_dot(first, self.low[...]))
-        mixed = (
+        return (
             products[0][:, :rows] - products[1][:, rows:],
             products[0][:, rows:] + products[1][:, :rows],
         )
+
+    def columns_stage(self, field, mixed):
+        piece, spaces = self.piece, self.spaces
         for target in range(spaces):
             for part in range(2):
                 self.out_chunks[field, target, part * piece:(part + 1) * piece, :] = mixed[part][target * piece:(target + 1) * piece]
@@ -198,8 +201,8 @@
     _, rows, width = probe_ref.shape
     mixer = Mixer(spaces, groups, width, rows, table_ref, scratch)
     mixer.enter()
-    mixer.columns_stage(0, probe_ref[0], probe_ref[1])
-    mixer.columns_stage(1, control_ref[0], control_ref[1])
+    mixer.columns_stage(0, mixer.columns_mix(mixer.vel, probe_ref[0], probe_ref[1]))
+    mixer.columns_stage(1, mixer.columns_mix(mixer.vel, control_ref[0], control_ref[1]))
     mixer.rows_stage(0)
     mixer.rows_stage(1)
     mixer.spread_stage(0)
@@ -209,35 +212,71 @@
     mixer.leave()
 
 
-def second_kernel(spaces, groups, probe_ref, control_ref, part_ref, table_ref, probe_out, control_out,
-                  core_part, far_parts, pair_sum, total, sum_send, sum_recv, *scratch):
+def second_kernel(spaces, groups, probe_ref, control_ref, part_ref, table_ref, chunks_out,
+                  core_part, own_mix, far_mix, far_in, sum_send, sum_recv, out_sems, *scratch):
     _, rows, width = probe_ref.shape
     mixer = Mixer(spaces, groups, width, rows, table_ref, scratch)
-    core, peer = mixer.core, {"vel": mixer.core_peer}
     mixer.enter()
-    swap = mixer.push(part_ref.at[1 - core], core_part, sum_send.at[0], sum_recv.at[0], peer)
-    mixer.columns_stage(0, control_ref[0], control_ref[1])
+    swap = mixer.push(part_ref, core_part, sum_send.at[0], sum_recv.at[0], {"vel": mixer.core_peer})
+    mixer.columns_stage(0, mixer.columns_mix(mixer.vel, control_ref[0], control_ref[1]))
     swap.wait_recv()
-    pair_sum[...] = part_ref[core] + core_part[...]
-    swaps = [
-        mixer.push(pair_sum, far_parts.at[far], sum_send.at[1 + far], sum_recv.at[1 + far], {"vel": mixer.far_peer(far)})
-        for far in range(1, groups // 2)
-    ]
+    core_part[...] = COUPLE * (core_part[...] + part_ref[...])
+    swaps = []
+    for far in range(1, groups // 2):
+        real, imag = mixer.columns_mix(mixer.far_peer(far), -core_part[1], core_part[0])
+        far_mix[far, 0] = real
+        far_mix[far, 1] = imag
+        swaps.append(mixer.push(
+            far_mix.at[far], far_in.at[far], sum_send.at[far], sum_recv.at[far], {"vel": mixer.far_peer(far)},
+        ))
+    real, imag = mixer.columns_mix(mixer.vel, probe_ref[0] - core_part[1], probe_ref[1] + core_part[0])
+    own_mix[0] = real
+    own_mix[1] = imag
     mixer.rows_stage(0)
-    whole = pair_sum[...]
+    whole = [own_mix[0], own_mix[1]]
     for far, copy in enumerate(swaps, 1):
         copy.wait_recv()
-        whole = whole + far_parts[far]
-    total[core] = whole
-    swap = mixer.push(total.at[core], total.at[core], sum_send.at[1], sum_recv.at[1], peer)
-    swap.wait_recv()
-    mixer.columns_stage(1, probe_ref[0] - COUPLE * total[1], probe_ref[1] + COUPLE * total[0])
+        whole = [whole[0] + far_in[far, 0], whole[1] + far_in[far, 1]]
+    mixer.columns_stage(1, whole)
     mixer.spread_stage(0)
+    control_copy = pltpu.make_async_copy(mixer.gathered.at[0], chunks_out.at[0], out_sems.at[0])
+    control_copy.start()
     mixer.rows_stage(1)
-    mixer.finish(0, control_out)
     mixer.spread_stage(1)
-    mixer.finish(1, probe_out)
+    probe_copy = pltpu.make_async_copy(mixer.gathered.at[1], chunks_out.at[1], out_sems.at[1])
+    probe_copy.start()
     mixer.leave()
+    control_copy.wait()
+    probe_copy.wait()
+
+
+def assemble_kernel(chunks_ref, control_out, probe_out):
+    _, _, spaces, tall, _ = chunks_ref.shape
+    piece = tall // 2
+    for field, out_ref in enumerate((control_out, probe_out)):
+        for start in range(0, spaces * piece, BAND):
+            for part in range(2):
+                block = jnp.concatenate([
+                    chunks_ref[field, 0, source, part * piece:(part + 1) * piece, :]
+                    for source in range(start // piece, (start + BAND) // piece)
+                ], axis=0)
+                out_ref[part, :, start:start + BAND] = block.T
+
+
+def assemble(chunks):
+    _, groups, spaces, tall, rows = chunks.shape
+    columns = spaces * tall // 2
+    shape = jax.ShapeDtypeStruct((2, rows, groups * columns), jnp.float32)
+    out = pl.BlockSpec((2, rows, columns), lambda i: (0, 0, i))
+    return pl.pallas_call(
+        assemble_kernel,
+        grid=(groups,),
+        in_specs=[pl.BlockSpec((2, 1, spaces, tall, rows), lambda i: (0, i, 0, 0, 0))],
+        out_specs=[out, out],
+        out_shape=[shape, shape],
+        compiler_params=pltpu.CompilerParams(vmem_limit_bytes=60 * 1024 * 1024),
+        name="assemble_fields",
+    )(chunks)
 
 
 def diffract(kernel, spaces, groups, collective, fields, extra, table):
@@ -254,23 +293,26 @@
         dma((2, groups // 2, spaces)), dma((2, groups // 2, spaces)),
         dma((2, groups // 2, spaces)), dma((2, groups // 2, spaces)),
     ]
+    shape = jax.ShapeDtypeStruct(fields[0].shape, jnp.float32)
+    vmem = pl.BlockSpec(memory_space=pltpu.VMEM)
+    out_shape, out_specs = [shape, shape], [vmem, vmem]
     if extra:
-        plane = pltpu.VMEM((rows, width), jnp.float32)
+        mixes = pltpu.VMEM((groups // 2, 2, width // groups, rows), jnp.float32)
         scratch = [
-            plane, pltpu.VMEM((groups // 2, rows, width), jnp.float32), plane,
             pltpu.VMEM((2, rows, width), jnp.float32),
-            dma((1 + groups // 2,)), dma((1 + groups // 2,)),
+            pltpu.VMEM((2, width // groups, rows), jnp.float32), mixes, mixes,
+            dma((groups // 2,)), dma((groups // 2,)), dma((2,)),
         ] + scratch
+        out_shape = jax.ShapeDtypeStruct((2, groups, spaces, 2 * piece, rows), jnp.float32)
+        out_specs = pl.BlockSpec(memory_space=pl.ANY)
     operands = (*fields, *extra, table)
-    vmem = pl.BlockSpec(memory_space=pltpu.VMEM)
-    shape = jax.ShapeDtypeStruct(fields[0].shape, jnp.float32)
     return pl.pallas_call(
         functools.partial(kernel, spaces, groups),
         in_specs=[vmem] * len(operands),
-        out_specs=[vmem, vmem],
-        out_shape=[shape, shape],
+        out_specs=out_specs,
+        out_shape=out_shape,
         scratch_shapes=scratch,
-        compiler_params=pltpu.CompilerParams(collective_id=collective, has_side_effects=True, vmem_limit_bytes=56 << 20),
+        compiler_params=pltpu.CompilerParams(collective_id=collective, has_side_effects=True, vmem_limit_bytes=60 * 1024 * 1024),
         name=kernel.__name__,
     )(*operands)
 
@@ -340,7 +382,7 @@
 
 def advance(optical, spin_part, probe_part, control, doppler, weight, gradient, scale):
     _, classes, rows, width = optical.shape
-    tall = 8
+    tall = min(16, rows)
     state = pl.BlockSpec((2, classes, tall, width), lambda i: (0, 0, i, 0))
     plane = pl.BlockSpec((2, tall, width), lambda i: (0, i, 0))
     small = pl.BlockSpec(memory_space=pltpu.SMEM)
@@ -354,7 +396,7 @@
             jax.ShapeDtypeStruct(spin_part.shape, jnp.float32),
             jax.ShapeDtypeStruct((2, rows, width), jnp.float32),
         ],
-        compiler_params=pltpu.CompilerParams(vmem_limit_bytes=40 << 20),
+        compiler_params=pltpu.CompilerParams(vmem_limit_bytes=60 * 1024 * 1024),
         name="advance_states",
     )(doppler, weight, probe_part, control, gradient, optical, spin_part)
 
@@ -382,7 +424,7 @@
         gradient_shift,
         1.0 / (optical_state.shape[1] * groups),
     )
-    probe_out, control_out = diffract(second_kernel, spaces, groups, 1, (probe_one, control_one), (weighted,), table)
+    control_out, probe_out = assemble(diffract(second_kernel, spaces, groups, 1, (probe_one, control_one), (weighted,), table))
     return (probe_out, control_out, optical_new, spin_new)
 
 

time: 141 us -> 131 us (0.929)
  local copies, waits for them, and re-layouts: 10.4 us -> 0 us
    unnamed x14 -> x0, local copies, waits for them, and re-layouts: 10.4 us -> none
    pallas_call x0 -> x1, Pallas kernels: none -> 3.98 us  [assemble(): pl.pallas_call(assemble_kernel, grid=(groups,), in_specs=[pl.BlockSpec((2...]
    pallas_call x2, Pallas kernels: 95.9 us -> 94.3 us  [diffract(): pl.pallas_call(functools.partial(kernel, spaces, groups), in_specs=[vmem]...]
where the time goes in v3:
time: 131 us
  Pallas kernels  130 us (99%)
    pallas_call x2, Pallas kernels, diffract(): pl.pallas_call(functools.partial(kernel, spaces, groups), in_specs=[vmem]...  94.3 us
    pallas_call x1, Pallas kernels, advance(): pl.pallas_call(functools.partial(state_kernel, scale=scale), grid=(rows /...  31.7 us
    pallas_call x1, Pallas kernels, assemble(): pl.pallas_call(assemble_kernel, grid=(groups,), in_specs=[pl.BlockSpec((2...  3.98 us

profile of v3, /device:TPU:0, one launch (start us, length us, event | category | flops | bytes accessed | tf_op | source)
XLA Modules:
  0.0 130.7 jit_solution(1180030092167234413)
XLA Ops:
  0.6 44.9 %first_kernel.1 = (f32[2,128,1024]{2,1,0:T(8,128)}, f32[2,128,1024]{2,1,0:T(8,128)}) custom-call(f32[2,128,1024]{2,1,0:T(8,128)} %probe_ref.1, f32[2,128,1024]{2,1,0:T(8,128)} %control_ref.1, bf16[2,2,128,2048]{3,2,1,0:T(8,128)(2,1)} %constant.2.clone.table_ref), custom_call_target="tpu_custom_call" | custom-call | tf_op jit(solution)/shard_map/first_kernel/pallas_call | solution.py:309
  45.6 31.7 %advance_states.1 = (f32[2,16,128,1024]{3,2,1,0:T(8,128)}, f32[2,16,128,1024]{3,2,1,0:T(8,128)}, f32[2,128,1024]{2,1,0:T(8,128)}) custom-call(f32[16]{0:T(128)} %doppler_ref.1, f32[16]{0:T(128)} %weight_ref.1, f32[2,128,1024]{2,1,0:T(8,128)} %get-tuple-element.11.probe_ref, f32[2,128,1024]{2,1,0:T(8,128)} %get-tuple-element.12.control_ref, ...), custom_call_target="tpu_custom_call" | custom-call | tf_op jit(solution)/shard_map/advance_states/pallas_call | solution.py:389
  77.3 49.4 %second_kernel.1.chunks_ref = f32[2,4,8,64,128]{4,3,2,1,0:T(8,128)} custom-call(f32[2,128,1024]{2,1,0:T(8,128)} %get-tuple-element.11.probe_ref, f32[2,128,1024]{2,1,0:T(8,128)} %get-tuple-element.12.control_ref, f32[2,128,1024]{2,1,0:T(8,128)} %get-tuple-element.13.part_ref, bf16[2,2,128,2048]{3,2,1,0:T(8,128)(2,1)} %constant.2.clone.table_ref), custom_call_target="tpu_custom_call" | custom-call | tf_op jit(solution)/shard_map/second_kernel/pallas_call | solution.py:309
  126.7 4.0 %assemble_fields.1 = (f32[2,128,1024]{2,1,0:T(8,128)}, f32[2,128,1024]{2,1,0:T(8,128)}) custom-call(f32[2,4,8,64,128]{4,3,2,1,0:T(8,128)} %second_kernel.1.chunks_ref), custom_call_target="tpu_custom_call" | custom-call | tf_op jit(solution)/shard_map/assemble_fields/pallas_call | solution.py:271

commit v4 on v3

--- a/solution.py
+++ b/solution.py
@@ -58,6 +58,13 @@
 
     def far_peer(self, hop):
         return ((self.far + hop) % (self.groups // 2)) * 2 + self.core
+
+    def back_source(self, hop):
+        members = 2 * BAND // self.rows
+        turns = self.spaces // members
+        turn, step = hop // members, hop % members
+        tile_index = (self.space // members + turns - turn) % turns
+        return tile_index * members + (self.space + members - step) % members
 
     def enter(self):
         barrier = pltpu.get_barrier_semaphore()
@@ -122,14 +129,16 @@
         high, low = split(values)
         stacked = jnp.concatenate([high, low], axis=0)
         tile = 2 * BAND
-        for start in range(0, width, tile):
+        members = tile // rows
+        self.back_in = getattr(self, "back_in", {})
+        self.back_in[field] = [None]
+        for turn in range(width // tile):
+            tile_index = (self.space // members + turn) % (width // tile)
             products = []
             for part in range(2):
                 bands = [
                     jnp.concatenate([
-                        self.table[part, level, :, width - block * BAND + start:width - block * BAND + start + tile]
-                        if width - block * BAND + start + tile <= 2 * width
-                        else self.table[part, level, :, start - block * BAND:start - block * BAND + tile]
+                        self.table[part, level, :, pl.ds(pl.multiple_of(width - block * BAND + tile_index * tile, BAND), tile)]
                         for block in range(width // BAND)
                     ], axis=0)
                     for level in range(2)
@@ -138,26 +147,26 @@
                 products.append(both[:2 * piece] + both[2 * piece:] + inner_dot(high, bands[1]))
             real = products[0][:piece] - products[1][piece:]
             imag = products[0][piece:] + products[1][:piece]
-            for offset in range(0, tile, rows):
-                target = (start + offset) // rows
-                self.back_chunks[field, target, :piece, :] = real[:, offset:offset + rows]
-                self.back_chunks[field, target, piece:, :] = imag[:, offset:offset + rows]
-        self.back_in = getattr(self, "back_in", {})
-        self.back_in[field] = []
-        for hop in range(1, spaces):
-            target = (self.space + hop) % spaces
-            self.back_in[field].append(self.push(
-                self.back_chunks.at[field, target], self.gathered.at[field, self.vel, self.space],
-                self.back_send.at[field, hop], self.back_recv.at[field, hop], {"space": target},
-            ))
+            for member in range(members):
+                target = tile_index * members + member
+                self.back_chunks[field, target, :piece, :] = real[:, member * rows:(member + 1) * rows]
+                self.back_chunks[field, target, piece:, :] = imag[:, member * rows:(member + 1) * rows]
+            for step in range(members):
+                hop = turn * members + step
+                if hop:
+                    target = tile_index * members + (self.space + step) % members
+                    self.back_in[field].append(self.push(
+                        self.back_chunks.at[field, target], self.gathered.at[field, self.vel, self.space],
+                        self.back_send.at[field, hop], self.back_recv.at[field, hop], {"space": target},
+                    ))
         self.gathered[field, self.vel, self.space] = self.back_chunks[field, self.space]
 
     def spread_stage(self, field):
         arrivals, core_copies = [], []
         for hop in range(self.spaces):
-            source = (self.space + self.spaces - hop) % self.spaces
+            source = self.back_source(hop)
             if hop:
-                self.back_in[field][hop - 1].wait_recv()
+                self.back_in[field][hop].wait_recv()
             chunk = self.gathered.at[field, self.vel, source]
             for far in range(1, self.groups // 2):
                 arrivals.append((far, hop, self.push(
@@ -170,7 +179,7 @@
             ))
         for far, hop, copy in arrivals:
             copy.wait_recv()
-            source = (self.space + self.spaces - hop) % self.spaces
+            source = self.back_source(hop)
             origin = self.far_peer(self.groups // 2 - far)
             chunk = self.gathered.at[field, origin, source]
             core_copies.append(self.push(

time: 131 us -> 130 us (level)
  no operation moved by 1% of the time
where the time goes in v4:
time: 130 us
  Pallas kernels  129 us (99%)
    pallas_call x2, Pallas kernels, diffract(): pl.pallas_call(functools.partial(kernel, spaces, groups), in_specs=[vmem]...  93.1 us
    pallas_call x1, Pallas kernels, advance(): pl.pallas_call(functools.partial(state_kernel, scale=scale), grid=(rows /...  31.9 us
    pallas_call x1, Pallas kernels, assemble(): pl.pallas_call(assemble_kernel, grid=(groups,), in_specs=[pl.BlockSpec((2...  3.98 us

profile of v4, /device:TPU:0, one launch (start us, length us, event | category | flops | bytes accessed | tf_op | source)
XLA Modules:
  0.0 129.6 jit_solution(16099675742939474194)
XLA Ops:
  0.6 44.1 %first_kernel.1 = (f32[2,128,1024]{2,1,0:T(8,128)}, f32[2,128,1024]{2,1,0:T(8,128)}) custom-call(f32[2,128,1024]{2,1,0:T(8,128)} %probe_ref.1, f32[2,128,1024]{2,1,0:T(8,128)} %control_ref.1, bf16[2,2,128,2048]{3,2,1,0:T(8,128)(2,1)} %constant.2.clone.table_ref), custom_call_target="tpu_custom_call" | custom-call | tf_op jit(solution)/shard_map/first_kernel/pallas_call | solution.py:318
  44.7 31.9 %advance_states.1 = (f32[2,16,128,1024]{3,2,1,0:T(8,128)}, f32[2,16,128,1024]{3,2,1,0:T(8,128)}, f32[2,128,1024]{2,1,0:T(8,128)}) custom-call(f32[16]{0:T(128)} %doppler_ref.1, f32[16]{0:T(128)} %weight_ref.1, f32[2,128,1024]{2,1,0:T(8,128)} %get-tuple-element.11.probe_ref, f32[2,128,1024]{2,1,0:T(8,128)} %get-tuple-element.12.control_ref, ...), custom_call_target="tpu_custom_call" | custom-call | tf_op jit(solution)/shard_map/advance_states/pallas_call | solution.py:398
  76.6 49.0 %second_kernel.1.chunks_ref = f32[2,4,8,64,128]{4,3,2,1,0:T(8,128)} custom-call(f32[2,128,1024]{2,1,0:T(8,128)} %get-tuple-element.11.probe_ref, f32[2,128,1024]{2,1,0:T(8,128)} %get-tuple-element.12.control_ref, f32[2,128,1024]{2,1,0:T(8,128)} %get-tuple-element.13.part_ref, bf16[2,2,128,2048]{3,2,1,0:T(8,128)(2,1)} %constant.2.clone.table_ref), custom_call_target="tpu_custom_call" | custom-call | tf_op jit(solution)/shard_map/second_kernel/pallas_call | solution.py:318
  125.7 4.0 %assemble_fields.1 = (f32[2,128,1024]{2,1,0:T(8,128)}, f32[2,128,1024]{2,1,0:T(8,128)}) custom-call(f32[2,4,8,64,128]{4,3,2,1,0:T(8,128)} %second_kernel.1.chunks_ref), custom_call_target="tpu_custom_call" | custom-call | tf_op jit(solution)/shard_map/assemble_fields/pallas_call | solution.py:280
